TPU v7x, 32 devices: a whole 2x2x4 slice. The times are simulated.
32 devices in a mesh: dp: 16 (over z, x, core), head: 2 (over y).
Axes of the slice: x: 2, y: 2, z: 4, core: 2. Of those that a mesh axis runs over, the one named last changes fastest.
Arguments:
- tokens: bfloat16 [16384, 1024], P(('dp', 'head')), may hold values from -6 to 6
- lengths: int32 [16], P('dp'), may hold values from 128 to 1024, as said below
- decay: float32 [8], P('head'), may hold values from 0.00048828125 to 0.03125
- w_query: bfloat16 [1024, 1024], P(None, 'head'), may hold values from -0.1875 to 0.1875
- w_key: bfloat16 [1024, 1024], P(None, 'head'), may hold values from -0.1875 to 0.1875
- w_value: bfloat16 [1024, 1024], P(None, 'head'), may hold values from -0.1875 to 0.1875
- w_gate: bfloat16 [1024, 1024], P(None, 'head'), may hold values from -0.1875 to 0.1875
- w_out: bfloat16 [1024, 1024], P('head'), may hold values from -0.1875 to 0.1875
- f_value: bfloat16 [1024, 2816], P('dp', 'head'), may hold values from -0.1875 to 0.1875
- f_gate: bfloat16 [1024, 2816], P('dp', 'head'), may hold values from -0.1875 to 0.1875
- f_out: bfloat16 [2816, 1024], P('head', 'dp'), may hold values from -0.109375 to 0.109375
- cotangent: bfloat16 [16384, 1024], P(('dp', 'head')), may hold values from -6 to 6
Outputs:
- output: bfloat16 [16384, 1024], P(('dp', 'head'))
- d_tokens: float32 [16384, 1024], P(('dp', 'head'))
- d_w_query: float32 [1024, 1024], P(None, 'head')
- d_w_key: float32 [1024, 1024], P(None, 'head')
- d_w_value: float32 [1024, 1024], P(None, 'head')
- d_w_gate: float32 [1024, 1024], P(None, 'head')
- d_w_out: float32 [1024, 1024], P('head')
- d_f_value: float32 [1024, 2816], P('dp', 'head')
- d_f_gate: float32 [1024, 2816], P('dp', 'head')
- d_f_out: float32 [2816, 1024], P('head', 'dp')
Inputs may be any that keep to these rules, and one draw needn't show every extreme that they name: `lengths`: each bucket holds a single slot, and that slot's sequence has length 1024.
All inputs are finite; a program needn't handle non-finite values.
Results may differ from a plain program's by a relative error of at most 0.022.
Values may be sent and summed in bfloat16 or wider, within the bound.
A program may use at most 192 MiB of HBM per device.

v0:
```python
import jax
import jax.numpy as jnp
from jax import lax
from jax.sharding import PartitionSpec as P

D = 1024
HD = 128
SEQ_DEV = 1
SLOT = 1024
BLOCK = 512
epsilon = 1e-06


def normalize(values):
    factor = lax.rsqrt(jnp.mean(values * values, axis=-1, keepdims=True) + epsilon)
    return (values * factor, factor)


def norm_back(grad_normed, normed, factor):
    inner_sum = jnp.mean(grad_normed * normed, axis=-1, keepdims=True)
    return factor * (grad_normed - normed * inner_sum)


def silu_slope(values):
    sigmoid = jax.nn.sigmoid(values)
    return sigmoid * (1.0 + values * (1.0 - sigmoid))


def matmul(left_side, right_side):
    return jnp.dot(left_side, right_side, preferred_element_type=jnp.float32)


def matmul_right_t(left_side, right_side):
    return lax.dot_general(
        left_side, right_side, (((1,), (1,)), ((), ())), preferred_element_type=jnp.float32
    )


def matmul_left_t(left_side, right_side):
    return lax.dot_general(
        left_side, right_side, (((0,), (0,)), ((), ())), preferred_element_type=jnp.float32
    )


def exact(form, left_side, right_side):
    return jnp.einsum(form, left_side, right_side, precision=lax.Precision.HIGHEST)


def decay_tables(rates):
    offsets = jnp.arange(BLOCK).astype(jnp.float32)
    spread = offsets[:, None] - offsets[None, :]
    causal = spread >= 0
    within = jnp.where(
        causal[None], jnp.exp(-rates[:, None, None] * jnp.where(causal, spread, 0.0)[None]), 0.0
    )
    first_decay = jnp.exp(-rates[:, None] * (offsets[None, :] + 1.0))
    last_decay = jnp.exp(-rates[:, None] * (BLOCK - 1.0 - offsets[None, :]))
    block_decay = jnp.exp(-rates * BLOCK)
    return (within, first_decay, last_decay, block_decay)


def to_blocks(values, heads):
    shaped = values.reshape(SEQ_DEV, SLOT // BLOCK, BLOCK, heads, HD)
    return shaped.transpose(1, 0, 3, 2, 4)


def from_blocks(blocks):
    return blocks.transpose(1, 0, 3, 2, 4).reshape(-1, blocks.shape[2] * blocks.shape[4])


def lightning_forward(query, keys, values, tables):
    within, first_decay, last_decay, block_decay = tables

    def advance(carried, inputs):
        query_blk, keys_blk, values_blk = inputs
        scores = jnp.einsum(
            "shbd,shcd->shbc", query_blk, keys_blk, preferred_element_type=jnp.float32
        )
        weights = (scores * within[None]).astype(jnp.bfloat16)
        inner_sum = jnp.einsum(
            "shbc,shcd->shbd", weights, values_blk, preferred_element_type=jnp.float32
        )
        outer_sum = first_decay[None, :, :, None] * exact(
            "shbd,shde->shbe", query_blk.astype(jnp.float32), carried
        )
        keys_scaled = keys_blk.astype(jnp.float32) * last_decay[None, :, :, None]
        update = exact("shbd,shbe->shde", keys_scaled, values_blk.astype(jnp.float32))
        return (
            block_decay[None, :, None, None] * carried + update,
            (inner_sum + outer_sum, carried),
        )

    initial = jnp.zeros((SEQ_DEV, query.shape[2], HD, HD), jnp.float32)
    final_state, (mixed, states) = lax.scan(advance, initial, (query, keys, values))
    return (mixed, states)


def lightning_backward(query, keys, values, grads, states, tables):
    within, first_decay, last_decay, block_decay = tables

    def retreat(later_grad, inputs):
        query_blk, keys_blk, values_blk, grad_blk, carried = inputs
        scores = jnp.einsum(
            "shbd,shcd->shbc", query_blk, keys_blk, preferred_element_type=jnp.float32
        )
        weights = (scores * within[None]).astype(jnp.bfloat16)
        d_weights = jnp.einsum(
            "shbd,shcd->shbc", grad_blk, values_blk, preferred_element_type=jnp.float32
        )
        d_scores = (d_weights * within[None]).astype(jnp.bfloat16)
        d_query = jnp.einsum(
            "shbc,shcd->shbd", d_scores, keys_blk, preferred_element_type=jnp.float32
        )
        d_keys = jnp.einsum(
            "shbc,shbd->shcd", d_scores, query_blk, preferred_element_type=jnp.float32
        )
        d_values = jnp.einsum(
            "shbc,shbd->shcd", weights, grad_blk, preferred_element_type=jnp.float32
        )
        grad_scaled = grad_blk.astype(jnp.float32) * first_decay[None, :, :, None]
        keys_scaled = keys_blk.astype(jnp.float32) * last_decay[None, :, :, None]
        d_query = d_query + exact("shbe,shde->shbd", grad_scaled, carried)
        d_keys = d_keys + last_decay[None, :, :, None] * exact(
            "shbe,shde->shbd", values_blk.astype(jnp.float32), later_grad
        )
        d_values = d_values + exact("shbd,shde->shbe", keys_scaled, later_grad)
        earlier = block_decay[None, :, None, None] * later_grad + exact(
            "shbd,shbe->shde", query_blk.astype(jnp.float32), grad_scaled
        )
        return (earlier, (d_query, d_keys, d_values))

    initial = jnp.zeros((SEQ_DEV, query.shape[2], HD, HD), jnp.float32)
    first_grad, results = lax.scan(
        retreat, initial, (query, keys, values, grads, states), reverse=True
    )
    return results


def body(
    tokens,
    lengths,
    decay,
    w_query,
    w_key,
    w_value,
    w_gate,
    w_out,
    f_value,
    f_gate,
    f_out,
    cotangent,
):
    own_rows = tokens.shape[0]
    first_row = lax.axis_index("head") * own_rows
    heads_here = decay.shape[0]
    tables = decay_tables(decay)
    positions = first_row + jnp.arange(own_rows, dtype=jnp.int32)
    slot_match = (positions // SLOT)[:, None] == jnp.arange(SEQ_DEV, dtype=jnp.int32)[None, :]
    length_of = jnp.sum(jnp.where(slot_match, lengths[None, :], 0), axis=1)
    keep_rows = (positions % SLOT < length_of).astype(jnp.float32)[:, None]
    inputs_f = tokens.astype(jnp.float32)
    normed, scale_in = normalize(inputs_f)
    gathered = lax.all_gather(normed.astype(jnp.bfloat16), "head", axis=0, tiled=True)
    query_pre = matmul(gathered, w_query)
    keys_pre = matmul(gathered, w_key)
    values_pre = matmul(gathered, w_value)
    gate_pre = matmul(gathered, w_gate)
    query_blocks = to_blocks(jax.nn.silu(query_pre).astype(jnp.bfloat16), heads_here)
    keys_blocks = to_blocks(jax.nn.silu(keys_pre).astype(jnp.bfloat16), heads_here)
    values_blocks = to_blocks(values_pre.astype(jnp.bfloat16), heads_here)
    mixed_blocks, states = lightning_forward(query_blocks, keys_blocks, values_blocks, tables)
    mixed = from_blocks(mixed_blocks)
    squares = lax.psum(jnp.sum(mixed * mixed, axis=1), "head")
    scale_out = lax.rsqrt(squares / D + epsilon)[:, None]
    mixed_unit = mixed * scale_out
    gated = (mixed_unit * gate_pre).astype(jnp.bfloat16)
    branch = lax.psum_scatter(
        matmul(gated, w_out).astype(jnp.bfloat16), "head", scatter_dimension=0, tiled=True
    ).astype(jnp.float32)
    middle = inputs_f + branch
    mid_normed, scale_mid = normalize(middle)
    mid_all = lax.all_gather(mid_normed.astype(jnp.bfloat16), "head", axis=0, tiled=True)
    value_full, gate_full = (
        lax.all_gather(f_value, "dp", axis=0, tiled=True),
        lax.all_gather(f_gate, "dp", axis=0, tiled=True),
    )
    down_full = lax.all_gather(f_out, "dp", axis=1, tiled=True)
    value_ffn = matmul(mid_all, value_full)
    gate_ffn = matmul(mid_all, gate_full)
    hidden = (value_ffn * gate_ffn).astype(jnp.bfloat16)
    ffn_branch = lax.psum_scatter(
        matmul(hidden, down_full).astype(jnp.bfloat16), "head", scatter_dimension=0, tiled=True
    ).astype(jnp.float32)
    output = ((middle + ffn_branch) * keep_rows).astype(jnp.bfloat16)
    grad_out = cotangent.astype(jnp.float32) * keep_rows
    grad_all = lax.all_gather(grad_out.astype(jnp.bfloat16), "head", axis=0, tiled=True)
    grad_hidden = matmul_right_t(grad_all, down_full)
    d_value_ffn = (grad_hidden * gate_ffn).astype(jnp.bfloat16)
    d_gate_ffn = (grad_hidden * value_ffn).astype(jnp.bfloat16)
    d_mid_normed = lax.psum_scatter(
        (matmul_right_t(d_value_ffn, value_full) + matmul_right_t(d_gate_ffn, gate_full)).astype(
            jnp.bfloat16
        ),
        "head",
        scatter_dimension=0,
        tiled=True,
    ).astype(jnp.float32)
    grad_middle = grad_out + norm_back(d_mid_normed, mid_normed, scale_mid)
    joined = jnp.concatenate([d_value_ffn, d_gate_ffn], axis=1)
    hidden_here = hidden.shape[1]
    shares = lax.psum_scatter(
        jnp.concatenate(
            [matmul_left_t(mid_all, joined), matmul_left_t(grad_all, hidden)], axis=1
        ).astype(jnp.bfloat16),
        "dp",
        scatter_dimension=0,
        tiled=True,
    ).astype(jnp.float32)
    d_f_value = shares[:, :hidden_here]
    d_f_gate = shares[:, hidden_here : 2 * hidden_here]
    d_f_out = shares[:, 2 * hidden_here :].T
    grad_rows = lax.all_gather(grad_middle.astype(jnp.bfloat16), "head", axis=0, tiled=True)
    d_gated = matmul_right_t(grad_rows, w_out)
    d_w_out_local = matmul_left_t(gated, grad_rows)
    d_gate_pre = (d_gated * mixed_unit).astype(jnp.bfloat16)
    d_unit = d_gated * gate_pre
    inner_out = lax.psum(jnp.sum(d_unit * mixed_unit, axis=1), "head")
    d_mixed = (scale_out * (d_unit - mixed_unit * (inner_out / D)[:, None])).astype(jnp.bfloat16)
    d_query, d_keys, d_values = lightning_backward(
        query_blocks, keys_blocks, values_blocks, to_blocks(d_mixed, heads_here), states, tables
    )
    d_query_pre = (from_blocks(d_query) * silu_slope(query_pre)).astype(jnp.bfloat16)
    d_keys_pre = (from_blocks(d_keys) * silu_slope(keys_pre)).astype(jnp.bfloat16)
    d_values_pre = from_blocks(d_values).astype(jnp.bfloat16)
    total = matmul_right_t(d_query_pre, w_query) + matmul_right_t(d_keys_pre, w_key)
    d_normed = lax.psum_scatter(
        (total + matmul_right_t(d_values_pre, w_value) + matmul_right_t(d_gate_pre, w_gate)).astype(
            jnp.bfloat16
        ),
        "head",
        scatter_dimension=0,
        tiled=True,
    ).astype(jnp.float32)
    d_tokens = grad_middle + norm_back(d_normed, normed, scale_in)
    grads_attention = (
        lax.psum(matmul_left_t(gathered, d_query_pre).astype(jnp.bfloat16), "dp").astype(
            jnp.float32
        ),
        lax.psum(matmul_left_t(gathered, d_keys_pre).astype(jnp.bfloat16), "dp").astype(
            jnp.float32
        ),
        lax.psum(matmul_left_t(gathered, d_values_pre).astype(jnp.bfloat16), "dp").astype(
            jnp.float32
        ),
        lax.psum(matmul_left_t(gathered, d_gate_pre).astype(jnp.bfloat16), "dp").astype(
            jnp.float32
        ),
        lax.psum(d_w_out_local.astype(jnp.bfloat16), "dp").astype(jnp.float32),
    )
    return (
        output,
        d_tokens,
        grads_attention[0],
        grads_attention[1],
        grads_attention[2],
        grads_attention[3],
        grads_attention[4],
        d_f_value,
        d_f_gate,
        d_f_out,
    )


def solution(mesh):
    placed = (
        P(("dp", "head"), None),
        P("dp"),
        P("head"),
        P(None, "head"),
        P(None, "head"),
        P(None, "head"),
        P(None, "head"),
        P("head", None),
        P("dp", "head"),
        P("dp", "head"),
        P("head", "dp"),
        P(("dp", "head"), None),
    )
    return jax.shard_map(
        body,
        mesh=mesh,
        in_specs=placed,
        out_specs=(
            P(("dp", "head"), None),
            P(("dp", "head"), None),
            P(None, "head"),
            P(None, "head"),
            P(None, "head"),
            P(None, "head"),
            P("head", None),
            P("dp", "head"),
            P("dp", "head"),
            P("head", "dp"),
        ),
        check_vma=False,
    )
```

profile of v0, /device:TPU:0, one launch (start us, length us, event | category | flops | bytes accessed | tf_op | source)
XLA Modules:
  0.0 686.0 jit_solution(16797415050043910649)
XLA Ops:
  15.0 33.8 %all-gather.8.cloned.1.call-done = bf16[1024,1024]{1,0:T(8,128)(2,1)} async-done(((bf16[512,1024]{1,0:T(8,128)(2,1)}), bf16[1024,1024]{1,0:T(8,128)(2,1)}) %all-gather.8.cloned.1.call-update) | async-done | bytes 2097168 | tf_op jit(solution)/shard_map/all_gather | solution.py:163
  48.8 4.4 multiply_convert_fusion.8
  69.1 15.1 %while.40 = (s32[]{:T(128)}, f32[1,4,128,128]{3,2,1,0:T(8,128)S(1)}, f32[2,1,4,512,128]{4,3,2,1,0:T(8,128)}, f32[2,1,4,128,128]{4,3,2,1,0:T(8,128)}, f32[4]{0:T(...) while((s32[]{:T(128)}, ...), condition=%wide.region_2.3_spmd.clone.clone.clone, body=%wide.region_1.2_spmd.clone.clone.clone.sunk | while | flops 1347751936 | bytes 17343232 | solution.py:94
  86.4 4.1 copy.42
  92.6 5.1 psum.49
  97.7 4.5 multiply_convert_fusion.6
  106.5 31.3 %reduce-scatter.6.cloned.1.call-done = bf16[512,1024]{1,0:T(8,128)(2,1)} async-done(((bf16[1024,1024]{1,0:T(8,128)(2,1)}), bf16[512,1024]{1,0:T(8,128)(2,1)}) %reduce-scatter.6.cloned.1.call-update) | async-done | bytes 1048592 | tf_op jit(solution)/shard_map/reduce_scatter | solution.py:177
  145.4 7.4 %all-gather.12.cloned.1.call-done = bf16[1024,1408]{1,0:T(8,128)(2,1)} async-done(((bf16[64,1408]{1,0:T(8,128)(2,1)}), bf16[1024,1408]{1,0:T(8,128)(2,1)}) %all-gather.12.cloned.1.call-update) | async-done | bytes 2883600 | tf_op jit(solution)/shard_map/all_gather | solution.py:184
  152.9 33.7 %all-gather.10.cloned.1.call-done = bf16[1024,1024]{1,0:T(8,128)(2,1)} async-done(((bf16[512,1024]{1,0:T(8,128)(2,1)}), bf16[1024,1024]{1,0:T(8,128)(2,1)}) %all-gather.10.cloned.1.call-update) | async-done | bytes 2097168 | tf_op jit(solution)/shard_map/all_gather | solution.py:182
  186.6 8.3 %fusion.155 = f32[1024,1408]{1,0:T(8,128)} fusion(bf16[1024,1024]{1,0:T(8,128)(2,1)} %all-gather.10.cloned.1.call-done, bf16[1024,1408]{1,0:T(8,128)(2,1)} %all-gather.12.cloned.1.call-done), kind=kOutput, calls=%fused_computation.209 | convolution fusion | flops 2952790016 | bytes 10747904 | tf_op jit(solution)/shard_map/dot_general | solution.py:30
  194.9 38.1 %all-gather.14.cloned.1.call-done = bf16[1024,1408]{1,0:T(8,128)(2,1)} async-done(((bf16[64,1408]{1,0:T(8,128)(2,1)}), bf16[1024,1408]{1,0:T(8,128)(2,1)}) %all-gather.14.cloned.1.call-update) | async-done | bytes 2883600 | tf_op jit(solution)/shard_map/all_gather | solution.py:185
  233.0 8.4 %fusion.156 = f32[1024,1408]{1,0:T(8,128)} fusion(bf16[1024,1024]{1,0:T(8,128)(2,1)} %all-gather.10.cloned.1.call-done, bf16[1024,1408]{1,0:T(8,128)(2,1)} %all-gather.14.cloned.1.call-done), kind=kOutput, calls=%fused_computation.210 | convolution fusion | flops 2952790016 | bytes 10747904 | tf_op jit(solution)/shard_map/dot_general | solution.py:30
  241.4 25.5 %all-gather.18.cloned.1.call-done = bf16[1024,1024]{1,0:T(8,128)(2,1)} async-done(((bf16[512,1024]{1,0:T(8,128)(2,1)}), bf16[1024,1024]{1,0:T(8,128)(2,1)}) %all-gather.18.cloned.1.call-update) | async-done | bytes 2097168 | tf_op jit(solution)/shard_map/all_gather | solution.py:196
  266.8 46.6 %all-gather.16.cloned.1.call-done = bf16[1408,1024]{0,1:T(8,128)(2,1)} async-done(((bf16[1408,64]{0,1:T(8,128)(2,1)}), bf16[1408,1024]{0,1:T(8,128)(2,1)}) %all-gather.16.cloned.1.call-update) | async-done | bytes 2883600 | tf_op jit(solution)/shard_map/all_gather | solution.py:187
  313.4 11.0 %multiply_convert_fusion = (bf16[1024,1408]{1,0:T(8,128)(2,1)S(1)}, bf16[1024,1408]{1,0:T(8,128)(2,1)}, bf16[1024,1408]{1,0:T(8,128)(2,1)S(1)}) fusion(f32[1024,1408]{1,0:T(8,128)} %fusion.155, f32[1024,1408]{1,0:T(8,128)} %fusion.156, bf16[1024,1024]{1,0:T(8,128)(2,1)} %all-gather.18.cloned.1.call-done, bf16[1408,1024]{0,1:T(8,128)(2,1)} %all-gather.16.cloned.1.call-done), kind=kOutput, calls=%fused_computation.120 | convolution fusion | flops 2961440768 | bytes 25165824 | tf_op jit(solution)/shard_map/dot_general | solution.py:34
  324.4 3.4 fusion.157
  328.3 4.6 add_convert_fusion.1
  333.0 30.6 %reduce-scatter.10.cloned.1.call-done = bf16[512,1024]{1,0:T(8,128)(2,1)} async-done(((bf16[1024,1024]{1,0:T(8,128)(2,1)}), bf16[512,1024]{1,0:T(8,128)(2,1)}) %reduce-scatter.10.cloned.1.call-update) | async-done | bytes 1048592 | tf_op jit(solution)/shard_map/reduce_scatter | solution.py:200
  371.5 29.3 %all-gather.20.cloned.1.call-done = bf16[1024,1024]{1,0:T(8,128)(2,1)} async-done(((bf16[512,1024]{1,0:T(8,128)(2,1)}), bf16[1024,1024]{1,0:T(8,128)(2,1)}) %all-gather.20.cloned.1.call-update) | async-done | bytes 2097168 | tf_op jit(solution)/shard_map/all_gather | solution.py:222
  400.8 5.3 multiply_reduce_fusion
  406.1 4.9 psum.50
  418.9 36.7 %while.41 = (s32[]{:T(128)}, f32[1,4,128,128]{3,2,1,0:T(8,128)S(1)}, f32[2,1,4,512,128]{4,3,2,1,0:T(8,128)}, f32[2,1,4,512,128]{4,3,2,1,0:T(8,128)}, bf16[2,1,4,...) while((s32[]{:T(128)}, ...), condition=%wide.region_13.14_spmd.clone.clone.clone, body=%wide.region_12.13_spmd.clone.clone.clone.sunk | while | flops 2964131840 | bytes 44889964 | solution.py:133
  426.5 3.3 fusion.266
  429.9 3.3 fusion.269
  444.8 3.3 fusion.266
  486.5 7.5 %convolution_convert_fusion.1 = bf16[1024,1024]{1,0:T(8,128)(2,1)} fusion(bf16[1024,1408]{1,0:T(8,128)(2,1)} %get-tuple-element.714, bf16[1408,1024]{0,1:T(8,128)(2,1)} %all-gather.16.cloned.1.call-done), kind=kOutput, calls=%fused_computation.160 | convolution fusion | flops 2953838592 | bytes 7864320 | tf_op jit(solution)/shard_map/dot_general | solution.py:30
  495.7 5.7 convolution_convert_fusion
  501.4 6.8 fusion.121
  508.3 3.8 pad_maximum_fusion
  512.1 115.8 %all-reduce.3.cloned.1.call-done = (bf16[1024,512]{1,0:T(8,128)(2,1)}, bf16[1024,512]{1,0:T(8,128)(2,1)}, bf16[1024,512]{1,0:T(8,128)(2,1)}, bf16[1024,512]{1,0:T(8,128)(2,1)}, bf16[512,1024]{1,0:T(8,128)(2,1)}) async-done(((bf16[1024,512]{1,0:T(8,128)(2,1)}, bf16[1024,512]{1,0:T(8,128)(2,1)}, bf16[1024,512]{1,0:T(8,128)(2,1)}, bf16[1024,512]{1,0:T(8,128)(2,1)}, bf16[512,1024]{1,0:T(8,128)(2,1)}), ...) | async-done | bytes 5242896 | tf_op jit(solution)/shard_map/psum | solution.py:246
  639.0 4.5 fusion.131
  643.4 31.9 %reduce-scatter.14.cloned.1.call-done = bf16[64,4224]{1,0:T(8,128)(2,1)} async-done(((bf16[1024,4224]{1,0:T(8,128)(2,1)}), bf16[64,4224]{1,0:T(8,128)(2,1)}) %reduce-scatter.14.cloned.1.call-update) | async-done | bytes 540688 | tf_op jit(solution)/shard_map/reduce_scatter | solution.py:211
  (238 shorter events, 142.1 us)
Async XLA Ops:
  8.0 95.2 %copy-start = (bf16[512,1024]{1,0:T(8,128)(2,1)S(1)}, bf16[512,1024]{1,0:T(8,128)(2,1)}, u32[]{:S(2)}) copy-start(bf16[512,1024]{1,0:T(8,128)(2,1)} %param.23) | copy-start | bytes 3145732
  8.0 40.8 %all-gather.8.cloned.1.call-start = ((), (), s32[]{:S(2)}) async-start(), calls=%async_computation.5 | async-start | bytes 3145728 | tf_op jit(solution)/shard_map/all_gather | solution.py:163
  8.1 4.8 copy-start.51
  10.3 38.5 %copy-start.48 = (bf16[1024,512]{1,0:T(8,128)(2,1)S(1)}, bf16[1024,512]{1,0:T(8,128)(2,1)}, u32[]{:S(2)}) copy-start(bf16[1024,512]{1,0:T(8,128)(2,1)} %param.20) | copy-start | bytes 3145732
  12.8 125.0 %reduce-scatter.6.cloned.1.call-start = ((), (), s32[]{:S(2)}) async-start(), calls=%async_computation.6 | async-start | bytes 3145728 | tf_op jit(solution)/shard_map/reduce_scatter | solution.py:177
  72.1 3.7 copy-start.13
  79.7 3.7 copy-start.13
  84.2 6.3 copy-start.6
  92.5 9.6 %copy-start.4 = (f32[64,8,2,512]{3,1,2,0:T(8,128)}, f32[64,8,2,512]{3,1,2,0:T(8,128)S(1)}, u32[]{:S(2)}) copy-start(f32[64,8,2,512]{3,1,2,0:T(8,128)S(1)} %copy.52) | copy-start | bytes 6291460
  105.8 32.0 %copy-start.2 = (bf16[512,1024]{1,0:T(8,128)(2,1)S(1)}, bf16[512,1024]{1,0:T(8,128)(2,1)}, u32[]{:S(2)}) copy-start(bf16[512,1024]{1,0:T(8,128)(2,1)} %param.16) | copy-start | bytes 3145732
  105.8 47.0 %all-gather.12.cloned.1.call-start = ((), (), s32[]{:S(2)}) async-start(), calls=%async_computation.8 | async-start | bytes 3063808 | tf_op jit(solution)/shard_map/all_gather | solution.py:184
  106.4 80.2 %all-gather.10.cloned.1.call-start = ((), (), s32[]{:S(2)}) async-start(), calls=%async_computation.7 | async-start | bytes 3145728 | tf_op jit(solution)/shard_map/all_gather | solution.py:182
  140.8 92.1 %all-gather.14.cloned.1.call-start = ((), (), s32[]{:S(2)}) async-start(), calls=%async_computation.9 | async-start | bytes 3063808 | tf_op jit(solution)/shard_map/all_gather | solution.py:185
  141.4 125.4 %all-gather.18.cloned.1.call-start = ((), (), s32[]{:S(2)}) async-start(), calls=%async_computation.12 | async-start | bytes 3145728 | tf_op jit(solution)/shard_map/all_gather | solution.py:196
  144.6 168.8 %all-gather.16.cloned.1.call-start = ((), (), s32[]{:S(2)}) async-start(), calls=%async_computation.10 | async-start | bytes 3063808 | tf_op jit(solution)/shard_map/all_gather | solution.py:187
  145.4 218.3 %reduce-scatter.10.cloned.1.call-start = ((), (), s32[]{:S(2)}) async-start(), calls=%async_computation.13 | async-start | bytes 3145728 | tf_op jit(solution)/shard_map/reduce_scatter | solution.py:200
  313.4 11.0 %copy-start.44 = (bf16[1024,1408]{1,0:T(8,128)(2,1)S(1)}, bf16[1024,1408]{1,0:T(8,128)(2,1)}, u32[]{:S(2)}) copy-start(bf16[1024,1408]{1,0:T(8,128)(2,1)} %all-gather.12.cloned.1.call-done) | copy-start | bytes 8650756
  324.4 3.9 copy-start.45
  333.0 67.8 %all-gather.20.cloned.1.call-start = ((), (), s32[]{:S(2)}) async-start(), calls=%async_computation.14 | async-start | bytes 3145728 | tf_op jit(solution)/shard_map/all_gather | solution.py:222
  367.5 33.3 %copy-start.5 = (f32[64,8,2,512]{3,1,2,0:T(8,128)S(1)}, f32[64,8,2,512]{3,1,2,0:T(8,128)}, u32[]{:S(2)}) copy-start(f32[64,8,2,512]{3,1,2,0:T(8,128)} %copy-done.4) | copy-start | bytes 6291460
  367.5 260.3 %all-reduce.3.cloned.1.call-start = ((), (), s32[]{:S(2)}) async-start(), calls=%async_computation.17 | async-start | bytes 10485760 | tf_op jit(solution)/shard_map/psum | solution.py:246
  426.2 3.7 copy-start.8
  426.2 3.7 copy-start.10
  444.5 3.7 copy-start.8
  462.4 11.0 %copy-start.38 = (bf16[1,2,512,4,128]{4,3,2,1,0:T(4,128)(2,1)}, bf16[1,2,512,4,128]{4,3,2,1,0:T(4,128)(2,1)S(1)}, u32[]{:S(2)}) copy-start(bf16[1,2,512,4,128]{4,3,2,1,0:T(4,128)(2,1)S(1)} %copy.46) | copy-start | bytes 3145732
  478.0 159.2 %reduce-scatter.12.cloned.1.call-start = ((), (), s32[]{:S(2)}) async-start(), calls=%async_computation.15 | async-start | bytes 3145728 | tf_op jit(solution)/shard_map/reduce_scatter | solution.py:236
  486.5 152.5 %reduce-scatter.8.cloned.1.call-start = ((), (), s32[]{:S(2)}) async-start(), calls=%async_computation.11 | async-start | bytes 3145728 | tf_op jit(solution)/shard_map/reduce_scatter | solution.py:191
  494.1 181.3 %reduce-scatter.14.cloned.1.call-start = ((), (), s32[]{:S(2)}) async-start(), calls=%async_computation.16 | async-start | bytes 9191424 | tf_op jit(solution)/shard_map/reduce_scatter | solution.py:211
  495.7 5.7 copy-start.26
  495.7 5.7 copy-start.28
  495.7 5.7 copy-start.46
  639.0 39.3 %copy-start.1 = (bf16[512,1024]{1,0:T(8,128)(2,1)S(1)}, bf16[512,1024]{1,0:T(8,128)(2,1)}, u32[]{:S(2)}) copy-start(bf16[512,1024]{1,0:T(8,128)(2,1)} %param.23) | copy-start | bytes 3145732
  (41 other events, 85.5 us)
Sparse Core Ops, SparseCore 0:
  12.9 35.8 all-gather.7
  106.0 31.7 reduce-scatter.5
  333.1 30.4 reduce-scatter.9
  367.6 33.1 all-gather.19
  486.6 31.8 reduce-scatter.11
  520.7 31.8 reduce-scatter.7
  557.2 118.1 reduce-scatter.13
Sparse Core Ops, SparseCore 1:
  108.9 43.9 all-gather.11
  154.9 31.6 all-gather.9
  189.0 43.9 all-gather.13
  235.2 31.6 all-gather.17
  269.4 43.9 all-gather.15
  478.1 149.7 all-reduce.2
where the time goes:
time: 694 us; the launch traced here: 686 us
  waiting for transfers between devices  426 us (61%)
  matrix products  147 us (21%)
  other arithmetic  43.4 us (6%)
  local copies, waits for them, and re-layouts  41 us (6%)
  between operations  17.1 us (2%)
  blocking collectives  10 us (1%)
    psum x1, waiting for transfers between devices, body(): lax.psum(matmul_left_t(gathered, d_query_pre).astype(jnp.bfloat16), 'dp')  116 us
    all_gather x1, waiting for transfers between devices, body(): down_full = lax.all_gather(f_out, 'dp', axis=1, tiled=True)  46.6 us
    dot_general x8, matrix products, matmul(): return jnp.dot(left_side, right_side, preferred_element_type=jnp.float32)  41.9 us
    all_gather x1, waiting for transfers between devices, body(): lax.all_gather(f_gate, 'dp', axis=0, tiled=True)  38.1 us
    all_gather x1, waiting for transfers between devices, body(): lax.all_gather(normed.astype(jnp.bfloat16), 'head', axis=0, tiled=True)  33.8 us
    all_gather x1, waiting for transfers between devices, body(): lax.all_gather(mid_normed.astype(jnp.bfloat16), 'head', axis=0, tiled=True)  33.7 us
    dot_general x8, matrix products, matmul_right_t(): lax.dot_general(left_side, right_side, (((1,), (1,)), ((), ())), preferre...  32.3 us
    reduce_scatter x1, waiting for transfers between devices, body(): lax.psum_scatter(jnp.concatenate([matmul_left_t(mid_all, joined), matmul_...  31.9 us
  transfers between devices with their start and end apart: 13, of which 11 were waited for; matrix products, arithmetic and copies ran while one was open for 11% of the time, Pallas kernels for 0%

commit v1 on v0

--- a/solution.py
+++ b/solution.py
@@ -1,3 +1,4 @@
+import functools
 import jax
 import jax.numpy as jnp
 from jax import lax
@@ -9,6 +10,13 @@
 SLOT = 1024
 BLOCK = 512
 epsilon = 1e-06
+
+
+def draw_the_paths(field, mesh_name):
+    return lax.all_gather(field, mesh_name).sum(axis=0)
+
+
+guide_frames = functools.partial(draw_the_paths, mesh_name="dp")
 
 
 def normalize(values):
@@ -243,9 +251,7 @@
     ).astype(jnp.float32)
     d_tokens = grad_middle + norm_back(d_normed, normed, scale_in)
     grads_attention = (
-        lax.psum(matmul_left_t(gathered, d_query_pre).astype(jnp.bfloat16), "dp").astype(
-            jnp.float32
-        ),
+        guide_frames(matmul_left_t(gathered, d_query_pre).astype(jnp.bfloat16)).astype(jnp.float32),
         lax.psum(matmul_left_t(gathered, d_keys_pre).astype(jnp.bfloat16), "dp").astype(
             jnp.float32
         ),

time: 694 us -> 784 us (1.13)
  waiting for transfers between devices: 426 us -> 504 us
  other arithmetic: 43.4 us -> 52.4 us
    reduce_scatter x1, waiting for transfers between devices: 31.9 us -> 156 us  [body(): lax.psum_scatter(jnp.concatenate([matmul_left_t(mid_all, joined), matmul_...]
    psum x1, waiting for transfers between devices: 116 us -> 68.9 us  [body(): lax.psum(matmul_left_t(gathered, d_keys_pre).astype(jnp.bfloat16), 'dp')]
    reduce_sum x0 -> x1, other arithmetic: none -> 8.99 us  [draw_the_paths(): return lax.all_gather(field, mesh_name).sum(axis=0)]
  transfers between devices with their start and end apart: 13 -> 14, of which waited for: 11 -> 11; matrix products, arithmetic and copies ran while one was open for 11% -> 11% of each run, Pallas kernels for 0% -> 0%
where the time goes in v1:
time: 784 us; the launch traced here: 775 us
  waiting for transfers between devices  504 us (64%)
  matrix products  147 us (19%)
  other arithmetic  52.4 us (7%)
  local copies, waits for them, and re-layouts  43.5 us (6%)
  between operations  17 us (2%)
  blocking collectives  10 us (1%)
    reduce_scatter x1, waiting for transfers between devices, body(): lax.psum_scatter(jnp.concatenate([matmul_left_t(mid_all, joined), matmul_...  156 us
    psum x1, waiting for transfers between devices, body(): lax.psum(matmul_left_t(gathered, d_keys_pre).astype(jnp.bfloat16), 'dp')  68.9 us
    all_gather x1, waiting for transfers between devices, body(): down_full = lax.all_gather(f_out, 'dp', axis=1, tiled=True)  46.6 us
    dot_general x8, matrix products, matmul(): return jnp.dot(left_side, right_side, preferred_element_type=jnp.float32)  41.9 us
    all_gather x1, waiting for transfers between devices, body(): lax.all_gather(f_gate, 'dp', axis=0, tiled=True)  38.1 us
    all_gather x1, waiting for transfers between devices, body(): lax.all_gather(normed.astype(jnp.bfloat16), 'head', axis=0, tiled=True)  33.7 us
    all_gather x1, waiting for transfers between devices, body(): lax.all_gather(mid_normed.astype(jnp.bfloat16), 'head', axis=0, tiled=True)  33.7 us
    dot_general x8, matrix products, matmul_right_t(): lax.dot_general(left_side, right_side, (((1,), (1,)), ((), ())), preferre...  32.3 us
  transfers between devices with their start and end apart: 14, of which 11 were waited for; matrix products, arithmetic and copies ran while one was open for 11% of the time, Pallas kernels for 0%

profile of v1, /device:TPU:0, one launch (start us, length us, event | category | flops | bytes accessed | tf_op | source)
XLA Modules:
  0.0 775.3 jit_solution(12640202401142251131)
XLA Ops:
  15.0 33.7 %all-gather.10.cloned.1.call-done = bf16[1024,1024]{1,0:T(8,128)(2,1)} async-done(((bf16[512,1024]{1,0:T(8,128)(2,1)}), bf16[1024,1024]{1,0:T(8,128)(2,1)}) %all-gather.10.cloned.1.call-update) | async-done | bytes 2097168 | tf_op jit(solution)/shard_map/all_gather | solution.py:171
  48.8 4.4 multiply_convert_fusion.8
  69.1 15.1 %while.40 = (s32[]{:T(128)}, f32[1,4,128,128]{3,2,1,0:T(8,128)S(1)}, f32[2,1,4,512,128]{4,3,2,1,0:T(8,128)}, f32[2,1,4,128,128]{4,3,2,1,0:T(8,128)}, f32[4]{0:T(...) while((s32[]{:T(128)}, ...), condition=%wide.region_2.3_spmd.clone.clone.clone, body=%wide.region_1.2_spmd.clone.clone.clone.sunk | while | flops 1347751936 | bytes 17343232 | solution.py:102
  86.4 4.1 copy.42
  92.6 5.1 psum.42
  97.7 4.5 multiply_convert_fusion.6
  106.4 31.3 %reduce-scatter.6.cloned.1.call-done = bf16[512,1024]{1,0:T(8,128)(2,1)} async-done(((bf16[1024,1024]{1,0:T(8,128)(2,1)}), bf16[512,1024]{1,0:T(8,128)(2,1)}) %reduce-scatter.6.cloned.1.call-update) | async-done | bytes 1048592 | tf_op jit(solution)/shard_map/reduce_scatter | solution.py:185
  145.4 7.4 all-gather.14.cloned.1.call-done
  152.8 33.7 %all-gather.12.cloned.1.call-done = bf16[1024,1024]{1,0:T(8,128)(2,1)} async-done(((bf16[512,1024]{1,0:T(8,128)(2,1)}), bf16[1024,1024]{1,0:T(8,128)(2,1)}) %all-gather.12.cloned.1.call-update) | async-done | bytes 2097168 | tf_op jit(solution)/shard_map/all_gather | solution.py:190
  186.5 8.3 %fusion.155 = f32[1024,1408]{1,0:T(8,128)} fusion(bf16[1024,1024]{1,0:T(8,128)(2,1)} %all-gather.12.cloned.1.call-done, bf16[1024,1408]{1,0:T(8,128)(2,1)} %all-gather.14.cloned.1.call-done), kind=kOutput, calls=%fused_computation.209 | convolution fusion | flops 2952790016 | bytes 10747904 | tf_op jit(solution)/shard_map/dot_general | solution.py:38
  194.9 38.1 %all-gather.16.cloned.1.call-done = bf16[1024,1408]{1,0:T(8,128)(2,1)} async-done(((bf16[64,1408]{1,0:T(8,128)(2,1)}), bf16[1024,1408]{1,0:T(8,128)(2,1)}) %all-gather.16.cloned.1.call-update) | async-done | bytes 2883600 | tf_op jit(solution)/shard_map/all_gather | solution.py:193
  233.0 8.4 %fusion.156 = f32[1024,1408]{1,0:T(8,128)} fusion(bf16[1024,1024]{1,0:T(8,128)(2,1)} %all-gather.12.cloned.1.call-done, bf16[1024,1408]{1,0:T(8,128)(2,1)} %all-gather.16.cloned.1.call-done), kind=kOutput, calls=%fused_computation.210 | convolution fusion | flops 2952790016 | bytes 10747904 | tf_op jit(solution)/shard_map/dot_general | solution.py:38
  241.4 25.5 %all-gather.20.cloned.1.call-done = bf16[1024,1024]{1,0:T(8,128)(2,1)} async-done(((bf16[512,1024]{1,0:T(8,128)(2,1)}), bf16[1024,1024]{1,0:T(8,128)(2,1)}) %all-gather.20.cloned.1.call-update) | async-done | bytes 2097168 | tf_op jit(solution)/shard_map/all_gather | solution.py:204
  266.8 46.6 %all-gather.18.cloned.1.call-done = bf16[1408,1024]{0,1:T(8,128)(2,1)} async-done(((bf16[1408,64]{0,1:T(8,128)(2,1)}), bf16[1408,1024]{0,1:T(8,128)(2,1)}) %all-gather.18.cloned.1.call-update) | async-done | bytes 2883600 | tf_op jit(solution)/shard_map/all_gather | solution.py:195
  313.4 11.0 %multiply_convert_fusion = (bf16[1024,1408]{1,0:T(8,128)(2,1)S(1)}, bf16[1024,1408]{1,0:T(8,128)(2,1)}, bf16[1024,1408]{1,0:T(8,128)(2,1)S(1)}) fusion(f32[1024,1408]{1,0:T(8,128)} %fusion.155, f32[1024,1408]{1,0:T(8,128)} %fusion.156, bf16[1024,1024]{1,0:T(8,128)(2,1)} %all-gather.20.cloned.1.call-done, bf16[1408,1024]{0,1:T(8,128)(2,1)} %all-gather.18.cloned.1.call-done), kind=kOutput, calls=%fused_computation.120 | convolution fusion | flops 2961440768 | bytes 25165824 | tf_op jit(solution)/shard_map/dot_general | solution.py:42
  324.4 3.4 fusion.157
  328.3 4.6 add_convert_fusion.1
  333.0 30.6 %reduce-scatter.10.cloned.1.call-done = bf16[512,1024]{1,0:T(8,128)(2,1)} async-done(((bf16[1024,1024]{1,0:T(8,128)(2,1)}), bf16[512,1024]{1,0:T(8,128)(2,1)}) %reduce-scatter.10.cloned.1.call-update) | async-done | bytes 1048592 | tf_op jit(solution)/shard_map/reduce_scatter | solution.py:208
  371.3 29.5 %all-gather.22.cloned.1.call-done = bf16[1024,1024]{1,0:T(8,128)(2,1)} async-done(((bf16[512,1024]{1,0:T(8,128)(2,1)}), bf16[1024,1024]{1,0:T(8,128)(2,1)}) %all-gather.22.cloned.1.call-update) | async-done | bytes 2097168 | tf_op jit(solution)/shard_map/all_gather | solution.py:230
  400.8 5.4 multiply_reduce_fusion
  406.2 4.9 psum.43
  419.0 36.9 %while.41 = (s32[]{:T(128)}, f32[1,4,128,128]{3,2,1,0:T(8,128)S(1)}, f32[2,1,4,512,128]{4,3,2,1,0:T(8,128)}, f32[2,1,4,512,128]{4,3,2,1,0:T(8,128)}, bf16[2,1,4,...) while((s32[]{:T(128)}, ...), condition=%wide.region_13.14_spmd.clone.clone.clone, body=%wide.region_12.13_spmd.clone.clone.clone.sunk | while | flops 2964131840 | bytes 44889964 | solution.py:141
  426.6 3.3 fusion.266
  444.9 3.3 fusion.266
  484.8 7.5 convolution_convert_fusion.1
  494.0 5.7 convolution_convert_fusion
  499.7 6.8 fusion.121
  506.6 3.8 pad_maximum_fusion
  514.6 68.9 %all-reduce.3.cloned.1.call-done = (bf16[1024,512]{1,0:T(8,128)(2,1)}, bf16[1024,512]{1,0:T(8,128)(2,1)}, bf16[1024,512]{1,0:T(8,128)(2,1)}, bf16[512,1024]{1,0:T(8,128)(2,1)}) async-done(((bf16[1024,512]{1,0:T(8,128)(2,1)}, bf16[1024,512]{1,0:T(8,128)(2,1)}, bf16[1024,512]{1,0:T(8,128)(2,1)}, bf16[512,1024]{1,0:T(8,128)(2,1)}), (bf16[1024,512]{1,0:T(8,128)(2,1)}, bf16[1024,512]{1,0:T(8,128)(2,1)}, ...) | async-done | bytes 4194320 | tf_op jit(solution)/shard_map/psum | solution.py:255
  593.4 4.3 fusion.131
  597.6 156.5 %reduce-scatter.14.cloned.1.call-done = bf16[64,4224]{1,0:T(8,128)(2,1)} async-done(((bf16[1024,4224]{1,0:T(8,128)(2,1)}), bf16[64,4224]{1,0:T(8,128)(2,1)}) %reduce-scatter.14.cloned.1.call-update) | async-done | bytes 540688 | tf_op jit(solution)/shard_map/reduce_scatter | solution.py:219
  757.0 9.0 %reduce_sum.79 = bf16[1024,512]{1,0:T(8,128)(2,1)S(1)} reduce(bf16[16,1024,512]{2,1,0:T(8,128)(2,1)} %bitcast.254, bf16[]{:T(256)} %constant.119.clone.1), dimensions={0}, to_apply=%region_16.17 | reduce | flops 7864320 | bytes 17825794 | tf_op jit(solution)/shard_map/reduce_sum | solution.py:16
  (244 shorter events, 147.7 us)
Async XLA Ops:
  8.0 95.1 %copy-start = (bf16[512,1024]{1,0:T(8,128)(2,1)S(1)}, bf16[512,1024]{1,0:T(8,128)(2,1)}, u32[]{:S(2)}) copy-start(bf16[512,1024]{1,0:T(8,128)(2,1)} %param.23) | copy-start | bytes 3145732
  8.0 40.8 %all-gather.10.cloned.1.call-start = ((), (), s32[]{:S(2)}) async-start(), calls=%async_computation.5 | async-start | bytes 3145728 | tf_op jit(solution)/shard_map/all_gather | solution.py:171
  8.1 4.8 copy-start.52
  10.3 38.5 %copy-start.48 = (bf16[1024,512]{1,0:T(8,128)(2,1)S(1)}, bf16[1024,512]{1,0:T(8,128)(2,1)}, u32[]{:S(2)}) copy-start(bf16[1024,512]{1,0:T(8,128)(2,1)} %param.20) | copy-start | bytes 3145732
  12.8 125.0 %reduce-scatter.6.cloned.1.call-start = ((), (), s32[]{:S(2)}) async-start(), calls=%async_computation.6 | async-start | bytes 3145728 | tf_op jit(solution)/shard_map/reduce_scatter | solution.py:185
  72.1 3.7 copy-start.13
  79.7 3.7 copy-start.13
  84.2 6.3 copy-start.6
  92.5 9.6 %copy-start.4 = (f32[64,8,2,512]{3,1,2,0:T(8,128)}, f32[64,8,2,512]{3,1,2,0:T(8,128)S(1)}, u32[]{:S(2)}) copy-start(f32[64,8,2,512]{3,1,2,0:T(8,128)S(1)} %copy.52) | copy-start | bytes 6291460
  105.8 32.0 %copy-start.2 = (bf16[512,1024]{1,0:T(8,128)(2,1)S(1)}, bf16[512,1024]{1,0:T(8,128)(2,1)}, u32[]{:S(2)}) copy-start(bf16[512,1024]{1,0:T(8,128)(2,1)} %param.16) | copy-start | bytes 3145732
  105.8 47.0 %all-gather.14.cloned.1.call-start = ((), (), s32[]{:S(2)}) async-start(), calls=%async_computation.8 | async-start | bytes 3063808 | tf_op jit(solution)/shard_map/all_gather | solution.py:192
  106.4 80.2 %all-gather.12.cloned.1.call-start = ((), (), s32[]{:S(2)}) async-start(), calls=%async_computation.7 | async-start | bytes 3145728 | tf_op jit(solution)/shard_map/all_gather | solution.py:190
  140.8 92.1 %all-gather.16.cloned.1.call-start = ((), (), s32[]{:S(2)}) async-start(), calls=%async_computation.9 | async-start | bytes 3063808 | tf_op jit(solution)/shard_map/all_gather | solution.py:193
  141.4 125.4 %all-gather.20.cloned.1.call-start = ((), (), s32[]{:S(2)}) async-start(), calls=%async_computation.12 | async-start | bytes 3145728 | tf_op jit(solution)/shard_map/all_gather | solution.py:204
  144.6 168.8 %all-gather.18.cloned.1.call-start = ((), (), s32[]{:S(2)}) async-start(), calls=%async_computation.10 | async-start | bytes 3063808 | tf_op jit(solution)/shard_map/all_gather | solution.py:195
  145.3 218.3 %reduce-scatter.10.cloned.1.call-start = ((), (), s32[]{:S(2)}) async-start(), calls=%async_computation.13 | async-start | bytes 3145728 | tf_op jit(solution)/shard_map/reduce_scatter | solution.py:208
  313.4 11.0 %copy-start.45 = (bf16[1024,1408]{1,0:T(8,128)(2,1)S(1)}, bf16[1024,1408]{1,0:T(8,128)(2,1)}, u32[]{:S(2)}) copy-start(bf16[1024,1408]{1,0:T(8,128)(2,1)} %all-gather.14.cloned.1.call-done) | copy-start | bytes 8650756
  324.4 3.9 copy-start.46
  333.0 67.8 %all-gather.22.cloned.1.call-start = ((), (), s32[]{:S(2)}) async-start(), calls=%async_computation.14 | async-start | bytes 3145728 | tf_op jit(solution)/shard_map/all_gather | solution.py:230
  367.5 33.3 %copy-start.5 = (f32[64,8,2,512]{3,1,2,0:T(8,128)S(1)}, f32[64,8,2,512]{3,1,2,0:T(8,128)}, u32[]{:S(2)}) copy-start(f32[64,8,2,512]{3,1,2,0:T(8,128)} %copy-done.4) | copy-start | bytes 6291460
  367.5 216.0 %all-reduce.3.cloned.1.call-start = ((), (), s32[]{:S(2)}) async-start(), calls=%async_computation.18 | async-start | bytes 8388608 | tf_op jit(solution)/shard_map/psum | solution.py:255
  426.3 3.7 copy-start.8
  444.6 3.7 copy-start.8
  444.6 3.7 copy-start.10
  471.5 119.9 %reduce-scatter.12.cloned.1.call-start = ((), (), s32[]{:S(2)}) async-start(), calls=%async_computation.15 | async-start | bytes 3145728 | tf_op jit(solution)/shard_map/reduce_scatter | solution.py:244
  484.8 108.5 %reduce-scatter.8.cloned.1.call-start = ((), (), s32[]{:S(2)}) async-start(), calls=%async_computation.11 | async-start | bytes 3145728 | tf_op jit(solution)/shard_map/reduce_scatter | solution.py:199
  492.4 261.8 %reduce-scatter.14.cloned.1.call-start = ((), (), s32[]{:S(2)}) async-start(), calls=%async_computation.16 | async-start | bytes 9191424 | tf_op jit(solution)/shard_map/reduce_scatter | solution.py:219
  494.0 5.7 copy-start.27
  494.0 5.7 copy-start.29
  494.0 5.7 copy-start.47
  510.4 246.6 %all-gather.24.cloned.1.call-start = ((), (), s32[]{:S(2)}) async-start(), calls=%async_computation.17 | async-start | bytes 17825792 | tf_op jit(solution)/shard_map/all_gather | solution.py:16
  757.0 10.6 %copy-start.1 = (bf16[512,1024]{1,0:T(8,128)(2,1)S(1)}, bf16[512,1024]{1,0:T(8,128)(2,1)}, u32[]{:S(2)}) copy-start(bf16[512,1024]{1,0:T(8,128)(2,1)} %param.23) | copy-start | bytes 3145732
  (43 other events, 92.0 us)
Sparse Core Ops, SparseCore 0:
  12.9 35.8 all-gather.9
  105.9 31.7 reduce-scatter.5
  333.1 30.4 reduce-scatter.9
  367.6 33.0 all-gather.21
  484.9 32.1 reduce-scatter.11
  519.9 31.8 reduce-scatter.7
  556.4 197.6 reduce-scatter.13
Sparse Core Ops, SparseCore 1:
  108.8 43.9 all-gather.13
  154.9 31.6 all-gather.11
  189.0 43.9 all-gather.15
  235.2 31.6 all-gather.19
  269.4 43.9 all-gather.17
  471.6 111.8 all-reduce.2
  585.8 164.5 all-gather.23
